TPU v7x, 256 devices: a whole 4x4x8 slice. The times are simulated.
256 devices in a mesh: row: 32 (over x_hi, z, core), col: 8 (over x_lo, y).
Axes of the slice: x: 4 (x_hi: 2, x_lo: 2; x = x_hi * 2 + x_lo), y: 4, z: 8, core: 2. Of those that a mesh axis runs over, the one named last changes fastest.
Arguments:
- amplitudes: float32 [1024, 64, 1200], P('col', 'row'), may hold values from -6 to 6
- integrals: float32 [64, 1200, 8, 1200], P('row', None, 'col'), may hold values from -0.09375 to 0.09375
- pair_energy: float32 [1024], P(('row', 'col')), may hold values from -4 to -1
- block_energy: float32 [8], replicated, may hold values from 0.2 to 3
- virtual_energy: float32 [1200], replicated, may hold values from 0.2 to 3
Outputs:
- new_amplitudes: float32 [1024, 8, 1200], P(('row', 'col'))
All inputs are finite; a program needn't handle non-finite values.
Results may differ from a plain program's by a relative error of at most 0.00027.
Values sent between devices are 32-bit elements; how exact they have to be, the bound alone decides.
A program may use at most 128 MiB of HBM per device.

v0:
```python
import jax
import jax.numpy as jnp
from jax import lax
from jax.sharding import PartitionSpec as P


def per_device(amplitudes, integrals, pair_energy, block_energy, virtual_energy):
    row_size = lax.axis_size("row")
    gathered = lax.all_gather(amplitudes, "col", axis=0, tiled=True)
    pair_count = gathered.shape[0]
    contract_len = gathered.shape[1] * gathered.shape[2]
    flattened = gathered.reshape(pair_count, contract_len)
    a_local = integrals.shape[2]
    virt_width = integrals.shape[3]
    weights = integrals.reshape(contract_len, a_local * virt_width)
    row_block = pair_count // row_size
    summed = lax.psum_scatter(
        jnp.dot(
            flattened, weights, precision=lax.Precision.HIGHEST, preferred_element_type=jnp.float32
        ),
        "row",
        scatter_dimension=0,
        tiled=True,
    )
    reshaped = summed.reshape(row_block, a_local, virt_width)
    arrived = lax.all_to_all(reshaped, "col", split_axis=0, concat_axis=1, tiled=True)
    denominator = (
        pair_energy[:, None, None] - block_energy[None, :, None] - virtual_energy[None, None, :]
    )
    return arrived / denominator


def solution(mesh):
    placed = (P("col", "row", None), P("row", None, "col", None), P(("row", "col")), P(), P())
    return jax.shard_map(
        per_device,
        mesh=mesh,
        in_specs=placed,
        out_specs=P(("row", "col"), None, None),
        check_vma=False,
    )
```

profile of v0, /device:TPU:4, one launch (start us, length us, event | category | flops | bytes accessed | tf_op | source)
XLA Modules:
  0.0 327.4 jit_solution(6195841070064501322)
XLA Ops:
  6.5 0.0 all-gather.2.cloned.1.call-start
  6.5 0.7 all-gather.2.cloned.1.call-update
  7.3 0.0 reduce-scatter.2.cloned.1.call-start
  7.3 9.8 %copy.10 = f32[2,1200,1,1200]{3,1,2,0:T(8,128)} copy(f32[2,1200,1,1200]{3,2,1,0:T(1,128)} %param.6) | data formatting | bytes 23040000
  17.1 109.0 %all-gather.2.cloned.1.call-done = f32[1024,2,1200]{0,2,1:T(8,128)} async-done(((f32[128,2,1200]{0,2,1:T(8,128)}), f32[1024,2,1200]{0,2,1:T(8,128)}) %all-gather.2.cloned.1.call-update) | async-done | bytes 9830416 | tf_op jit(solution)/shard_map/all_gather | solution.py:9
  126.1 0.0 copy-start.1
  126.1 0.0 copy-start.2
  126.1 0.0 copy-start
  126.1 47.6 %fusion = f32[1024,1200]{1,0:T(8,128)} fusion(f32[1024,2400]{0,1:T(8,128)} %bitcast.13, f32[2400,1200]{1,0:T(8,128)} %bitcast.10), kind=kOutput, calls=%fused_computation.2 | convolution fusion | flops 35389440000 | bytes 26265600 | tf_op jit(solution)/shard_map/dot_general | solution.py:18
  173.7 0.0 reduce-scatter.2.cloned.1.call-update
  173.7 132.8 %reduce-scatter.2.cloned.1.call-done = f32[32,1200]{1,0:T(8,128)} async-done(((f32[1024,1200]{1,0:T(8,128)}), f32[32,1200]{1,0:T(8,128)}) %reduce-scatter.2.cloned.1.call-update) | async-done | bytes 153616 | tf_op jit(solution)/shard_map/reduce_scatter | solution.py:17
  306.5 1.7 copy.8
  308.2 4.8 %all-to-all-start = ((f32[32,1,1200]{2,1,0:T(1,128)}), f32[32,1,1200]{2,1,0:T(1,128)S(1)}, u32[]{:S(2)}, u32[]{:S(2)}) async-start(f32[32,1,1200]{2,1,0:T(1,128)} %copy.8), calls=%async_computation.1 | async-start | bytes 327680 | tf_op jit(solution)/shard_map/all_to_all | solution.py:26
  313.1 0.0 copy-done.1
  313.1 0.0 copy-done.2
  313.1 0.1 broadcast_subtract_fusion
  313.2 6.7 %all-to-all-done = f32[32,1,1200]{2,1,0:T(1,128)S(1)} async-done(((f32[32,1,1200]{2,1,0:T(1,128)}), f32[32,1,1200]{2,1,0:T(1,128)S(1)}, u32[]{:S(2)}, u32[]{:S(2)}) %all-to-all-start) | async-done | bytes 153632 | tf_op jit(solution)/shard_map/all_to_all | solution.py:26
  319.8 0.0 copy-done
  319.8 0.8 bitcast_divide_fusion
Async XLA Ops:
  6.5 119.5 %all-gather.2.cloned.1.call-start = ((), (), s32[]{:S(2)}) async-start(), calls=%async_computation.2 | async-start | bytes 11059200 | tf_op jit(solution)/shard_map/all_gather | solution.py:9
  7.3 299.2 %reduce-scatter.2.cloned.1.call-start = ((), (), s32[]{:S(2)}) async-start(), calls=%async_computation.3 | async-start | bytes 5406720 | tf_op jit(solution)/shard_map/reduce_scatter | solution.py:17
  126.1 187.0 %copy-start.1 = (f32[8]{0:T(128)S(1)}, f32[8]{0:T(128)}, u32[]{:S(2)}) copy-start(f32[8]{0:T(128)} %param.8) | copy-start | bytes 100
  126.1 187.0 %copy-start.2 = (f32[4]{0:T(128)S(1)}, f32[4]{0:T(128)}, u32[]{:S(2)}) copy-start(f32[4]{0:T(128)} %param.7) | copy-start | bytes 52
  126.1 193.7 %copy-start = (f32[1200]{0:T(1024)S(1)}, f32[1200]{0:T(1024)}, u32[]{:S(2)}) copy-start(f32[1200]{0:T(1024)} %param.9) | copy-start | bytes 14404
  308.2 11.6 %all-to-all-start = ((f32[32,1,1200]{2,1,0:T(1,128)}), f32[32,1,1200]{2,1,0:T(1,128)S(1)}, u32[]{:S(2)}, u32[]{:S(2)}) async-start(f32[32,1,1200]{2,1,0:T(1,128)} %copy.8), calls=%async_computation.1 | async-start | bytes 327680 | tf_op jit(solution)/shard_map/all_to_all | solution.py:26
Sparse Core Ops, SparseCore 0:
  9.1 116.9 all-gather.1
  173.8 132.6 reduce-scatter.1
where the time goes:
time: 328 us; the launch traced here: 327 us
  waiting for transfers between devices  249 us (76%)
  matrix products  47.6 us (15%)
  between operations  13.4 us (4%)
  local copies, waits for them, and re-layouts  11.5 us (4%)
  starting transfers between devices  4.87 us (1%)
    reduce_scatter x1, waiting for transfers between devices, per_device(): lax.psum_scatter(jnp.dot(flattened, weights, precision=lax.Precision.HIGH...  133 us
    all_gather x1, waiting for transfers between devices, per_device(): gathered = lax.all_gather(amplitudes, 'col', axis=0, tiled=True)  109 us
    dot_general x1, matrix products, per_device(): jnp.dot(flattened, weights, precision=lax.Precision.HIGHEST, preferred_el...  47.6 us
    unnamed x7, local copies, waits for them, and re-layouts  9.78 us
    all_to_all x1, waiting for transfers between devices, per_device(): lax.all_to_all(reshaped, 'col', split_axis=0, concat_axis=1, tiled=True)  6.67 us
  transfers between devices with their start and end apart: 3, of which 3 were waited for; matrix products, arithmetic and copies ran while one was open for 3% of the time, Pallas kernels for 0%

commit v1 on v0

--- a/solution.py
+++ b/solution.py
@@ -23,7 +23,10 @@
         tiled=True,
     )
     reshaped = summed.reshape(row_block, a_local, virt_width)
-    arrived = lax.all_to_all(reshaped, "col", split_axis=0, concat_axis=1, tiled=True)
+    arrived = jnp.concatenate(
+        lax.all_to_all(jnp.stack(jnp.split(reshaped, lax.axis_size("col"), axis=0)), "col", 0, 0),
+        axis=1,
+    )
     denominator = (
         pair_energy[:, None, None] - block_energy[None, :, None] - virtual_energy[None, None, :]
     )

time: 328 us -> 338 us (1.030)
  local copies, waits for them, and re-layouts: 11.5 us -> 21.6 us
    unnamed x7 -> x14, local copies, waits for them, and re-layouts: 9.78 us -> 19.5 us
where the time goes in v1:
time: 338 us; the launch traced here: 337 us
  waiting for transfers between devices  249 us (74%)
  matrix products  47.6 us (14%)
  local copies, waits for them, and re-layouts  21.6 us (6%)
  between operations  13.4 us (4%)
  starting transfers between devices  4.87 us (1%)
    reduce_scatter x1, waiting for transfers between devices, per_device(): lax.psum_scatter(jnp.dot(flattened, weights, precision=lax.Precision.HIGH...  133 us
    all_gather x1, waiting for transfers between devices, per_device(): gathered = lax.all_gather(amplitudes, 'col', axis=0, tiled=True)  109 us
    dot_general x1, matrix products, per_device(): jnp.dot(flattened, weights, precision=lax.Precision.HIGHEST, preferred_el...  47.6 us
    unnamed x14, local copies, waits for them, and re-layouts  19.5 us
  transfers between devices with their start and end apart: 3, of which 3 were waited for; matrix products, arithmetic and copies ran while one was open for 3% of the time, Pallas kernels for 0%

profile of v1, /device:TPU:4, one launch (start us, length us, event | category | flops | bytes accessed | tf_op | source)
XLA Modules:
  0.0 336.8 jit_solution(9526004845052984429)
XLA Ops:
  6.5 0.0 all-gather.2.cloned.1.call-start
  6.5 0.7 all-gather.2.cloned.1.call-update
  7.3 0.0 reduce-scatter.2.cloned.1.call-start
  7.3 9.8 %copy.8 = f32[2,1200,1,1200]{3,1,2,0:T(8,128)} copy(f32[2,1200,1,1200]{3,2,1,0:T(1,128)} %param.6) | data formatting | bytes 23040000
  17.1 109.0 %all-gather.2.cloned.1.call-done = f32[1024,2,1200]{0,2,1:T(8,128)} async-done(((f32[128,2,1200]{0,2,1:T(8,128)}), f32[1024,2,1200]{0,2,1:T(8,128)}) %all-gather.2.cloned.1.call-update) | async-done | bytes 9830416 | tf_op jit(solution)/shard_map/all_gather | solution.py:9
  126.1 0.0 copy-start.1
  126.1 0.0 copy-start.2
  126.1 0.0 copy-start
  126.1 47.6 %fusion.8 = f32[1024,1200]{1,0:T(8,128)} fusion(f32[1024,2400]{0,1:T(8,128)} %bitcast.41, f32[2400,1200]{1,0:T(8,128)} %bitcast.40), kind=kOutput, calls=%fused_computation.18 | convolution fusion | flops 35389440000 | bytes 26265600 | tf_op jit(solution)/shard_map/dot_general | solution.py:18
  173.7 0.0 reduce-scatter.2.cloned.1.call-update
  173.7 132.8 %reduce-scatter.2.cloned.1.call-done = f32[32,1200]{1,0:T(8,128)} async-done(((f32[1024,1200]{1,0:T(8,128)}), f32[32,1200]{1,0:T(8,128)}) %reduce-scatter.2.cloned.1.call-update) | async-done | bytes 153616 | tf_op jit(solution)/shard_map/reduce_scatter | solution.py:17
  306.5 1.4 fusion.7
  307.9 1.4 fusion.6
  309.3 1.4 fusion.5
  310.7 1.4 fusion.4
  312.0 1.4 fusion.3
  313.4 1.4 fusion.2
  314.8 1.4 fusion.1
  316.2 1.4 fusion
  317.6 4.8 %all-to-all-start = ((f32[8,4,1,1200]{3,1,2,0:T(4,128)}), f32[8,4,1,1200]{3,1,2,0:T(4,128)S(1)}, u32[]{:S(2)}, u32[]{:S(2)}) async-start(f32[8,4,1,1200]{3,1,2,0:T(4,128)} %fusion), calls=%async_computation.1 | async-start | bytes 327680 | tf_op jit(solution)/shard_map/all_to_all | solution.py:27
  322.4 0.0 copy-done.1
  322.4 0.0 copy-done.2
  322.4 0.1 broadcast_subtract_fusion
  322.5 6.7 %all-to-all-done = f32[8,4,1,1200]{3,1,2,0:T(4,128)S(1)} async-done(((f32[8,4,1,1200]{3,1,2,0:T(4,128)}), f32[8,4,1,1200]{3,1,2,0:T(4,128)S(1)}, u32[]{:S(2)}, u32[]{:S(2)}) %all-to-all-start) | async-done | bytes 153632 | tf_op jit(solution)/shard_map/all_to_all | solution.py:27
  329.2 0.0 copy-done
  329.2 0.1 bitcast_divide_fusion
  329.3 0.7 copy.7
Async XLA Ops:
  6.5 119.5 %all-gather.2.cloned.1.call-start = ((), (), s32[]{:S(2)}) async-start(), calls=%async_computation.2 | async-start | bytes 11059200 | tf_op jit(solution)/shard_map/all_gather | solution.py:9
  7.3 299.2 %reduce-scatter.2.cloned.1.call-start = ((), (), s32[]{:S(2)}) async-start(), calls=%async_computation.3 | async-start | bytes 5406720 | tf_op jit(solution)/shard_map/reduce_scatter | solution.py:17
  126.1 196.4 %copy-start.1 = (f32[8]{0:T(128)S(1)}, f32[8]{0:T(128)}, u32[]{:S(2)}) copy-start(f32[8]{0:T(128)} %param.8) | copy-start | bytes 100
  126.1 196.4 %copy-start.2 = (f32[4]{0:T(128)S(1)}, f32[4]{0:T(128)}, u32[]{:S(2)}) copy-start(f32[4]{0:T(128)} %param.7) | copy-start | bytes 52
  126.1 203.1 %copy-start = (f32[1200]{0:T(1024)S(1)}, f32[1200]{0:T(1024)}, u32[]{:S(2)}) copy-start(f32[1200]{0:T(1024)} %param.9) | copy-start | bytes 14404
  317.6 11.6 %all-to-all-start = ((f32[8,4,1,1200]{3,1,2,0:T(4,128)}), f32[8,4,1,1200]{3,1,2,0:T(4,128)S(1)}, u32[]{:S(2)}, u32[]{:S(2)}) async-start(f32[8,4,1,1200]{3,1,2,0:T(4,128)} %fusion), calls=%async_computation.1 | async-start | bytes 327680 | tf_op jit(solution)/shard_map/all_to_all | solution.py:27
Sparse Core Ops, SparseCore 0:
  9.1 116.9 all-gather.1
  173.8 132.6 reduce-scatter.1

commit v2 on v0

--- a/solution.py
+++ b/solution.py
@@ -6,7 +6,9 @@
 
 def per_device(amplitudes, integrals, pair_energy, block_energy, virtual_energy):
     row_size = lax.axis_size("row")
-    gathered = lax.all_gather(amplitudes, "col", axis=0, tiled=True)
+    gathered = jnp.concatenate(
+        lax.all_to_all(jnp.stack([amplitudes] * lax.axis_size("col")), "col", 0, 0), axis=0
+    )
     pair_count = gathered.shape[0]
     contract_len = gathered.shape[1] * gathered.shape[2]
     flattened = gathered.reshape(pair_count, contract_len)

time: 328 us -> 372 us (1.13)
  matrix products: 47.6 us -> 82.1 us
  local copies, waits for them, and re-layouts: 11.5 us -> 26.8 us
  waiting for transfers between devices: 249 us -> 239 us
  starting transfers between devices: 4.87 us -> 9.93 us
    all_gather x1 -> x0, waiting for transfers between devices: 109 us -> none  [per_device(): gathered = lax.all_gather(amplitudes, 'col', axis=0, tiled=True)]
    all_to_all x0 -> x1, waiting for transfers between devices: none -> 99.4 us  [per_device(): lax.all_to_all(jnp.stack([amplitudes] * lax.axis_size('col')), 'col', 0, 0)]
    dot_general x1, matrix products: 47.6 us -> 82.1 us  [per_device(): jnp.dot(flattened, weights, precision=lax.Precision.HIGHEST, preferred_el...]
    all_to_all x0 -> x1, local copies, waits for them, and re-layouts: none -> 9.54 us  [per_device(): lax.all_to_all(jnp.stack([amplitudes] * lax.axis_size('col')), 'col', 0, 0)]
    another operation x0 -> x1, local copies, waits for them, and re-layouts: none -> 5.68 us  [per_device(): jnp.stack([amplitudes] * lax.axis_size('col'))]
    all_to_all x0 -> x1, starting transfers between devices: none -> 5.15 us  [per_device(): lax.all_to_all(jnp.stack([amplitudes] * lax.axis_size('col')), 'col', 0, 0)]
    unnamed x7 -> x9, local copies, waits for them, and re-layouts: 9.78 us -> 9.79 us
where the time goes in v2:
time: 372 us
  waiting for transfers between devices  239 us (64%)
  matrix products  82.1 us (22%)
  local copies, waits for them, and re-layouts  26.8 us (7%)
  between operations  13.5 us (4%)
  starting transfers between devices  9.93 us (3%)
    reduce_scatter x1, waiting for transfers between devices, per_device(): lax.psum_scatter(jnp.dot(flattened, weights, precision=lax.Precision.HIGH...  133 us
    all_to_all x1, waiting for transfers between devices, per_device(): lax.all_to_all(jnp.stack([amplitudes] * lax.axis_size('col')), 'col', 0, 0)  99.4 us
    dot_general x1, matrix products, per_device(): jnp.dot(flattened, weights, precision=lax.Precision.HIGHEST, preferred_el...  82.1 us
    unnamed x9, local copies, waits for them, and re-layouts  9.79 us
    all_to_all x1, local copies, waits for them, and re-layouts, per_device(): lax.all_to_all(jnp.stack([amplitudes] * lax.axis_size('col')), 'col', 0, 0)  9.54 us
  transfers between devices with their start and end apart: 3, of which 3 were waited for; matrix products, arithmetic and copies ran while one was open for 3% of the time, Pallas kernels for 0%

profile of v2, /device:TPU:4, one launch (start us, length us, event | category | flops | bytes accessed | tf_op | source)
XLA Modules:
  0.0 372.1 jit_solution(11598209096059715557)
XLA Ops:
  6.5 5.7 %stack.2 = f32[8,128,2,1200]{1,3,2,0:T(8,128)} broadcast(f32[128,2,1200]{0,2,1:T(8,128)} %param.5), dimensions={1,2,3} | broadcast | bytes 11059200 | tf_op jit(solution)/shard_map/stack | solution.py:10
  12.2 5.1 %all-to-all-start = ((f32[8,128,2,1200]{1,3,2,0:T(8,128)}), f32[8,128,2,1200]{1,3,2,0:T(8,128)}, u32[]{:S(2)}, u32[]{:S(2)}) async-start(f32[8,128,2,1200]{1,3,2,0:T(8,128)} %stack.2), calls=%async_computation | async-start | bytes 19660800 | tf_op jit(solution)/shard_map/all_to_all | solution.py:10
  17.4 0.0 reduce-scatter.2.cloned.1.call-start
  17.4 9.8 %copy.12 = f32[2,1200,1,1200]{3,1,2,0:T(8,128)} copy(f32[2,1200,1,1200]{3,2,1,0:T(1,128)} %param.6) | data formatting | bytes 23040000
  27.2 99.4 %all-to-all-done = f32[8,128,2,1200]{1,3,2,0:T(8,128)} async-done(((f32[8,128,2,1200]{1,3,2,0:T(8,128)}), f32[8,128,2,1200]{1,3,2,0:T(8,128)}, u32[]{:S(2)}, u32[]{:S(2)}) %all-to-all-start) | async-done | bytes 9830432 | tf_op jit(solution)/shard_map/all_to_all | solution.py:10
  126.6 0.0 copy-start
  126.6 9.5 %copy.9 = f32[8,128,2,1200]{1,0,3,2:T(8,128)S(1)} copy(f32[8,128,2,1200]{1,3,2,0:T(8,128)} %all-to-all-done) | data formatting | bytes 19660800 | tf_op jit(solution)/shard_map/all_to_all | solution.py:10
  136.1 0.0 copy-done
  136.1 0.0 copy-start.2
  136.1 0.0 copy-start.3
  136.1 0.0 copy-start.1
  136.2 82.1 %fusion = f32[1024,1200]{1,0:T(8,128)} fusion(f32[2400,1200]{1,0:T(8,128)S(1)} %bitcast.15, f32[300,8,8,128]{3,2,1,0:T(8,128)S(1)} %bitcast.16), kind=kOutput, calls=%fused_computation | convolution fusion | flops 35389440000 | bytes 26265600 | tf_op jit(solution)/shard_map/dot_general | solution.py:20
  218.2 0.0 reduce-scatter.2.cloned.1.call-update
  218.3 133.0 %reduce-scatter.2.cloned.1.call-done = f32[32,1200]{1,0:T(8,128)} async-done(((f32[1024,1200]{1,0:T(8,128)}), f32[32,1200]{1,0:T(8,128)}) %reduce-scatter.2.cloned.1.call-update) | async-done | bytes 153616 | tf_op jit(solution)/shard_map/reduce_scatter | solution.py:19
  351.3 1.7 copy.10
  353.0 4.7 %all-to-all-start.1 = ((f32[32,1,1200]{2,1,0:T(1,128)}), f32[32,1,1200]{2,1,0:T(1,128)S(1)}, u32[]{:S(2)}, u32[]{:S(2)}) async-start(f32[32,1,1200]{2,1,0:T(1,128)} %copy.10), calls=%async_computation.2 | async-start | bytes 327680 | tf_op jit(solution)/shard_map/all_to_all | solution.py:28
  357.8 0.0 copy-done.2
  357.8 0.0 copy-done.3
  357.8 0.1 broadcast_subtract_fusion
  357.9 6.7 %all-to-all-done.1 = f32[32,1,1200]{2,1,0:T(1,128)S(1)} async-done(((f32[32,1,1200]{2,1,0:T(1,128)}), f32[32,1,1200]{2,1,0:T(1,128)S(1)}, u32[]{:S(2)}, u32[]{:S(2)}) %all-to-all-start.1) | async-done | bytes 153632 | tf_op jit(solution)/shard_map/all_to_all | solution.py:28
  364.5 0.0 copy-done.1
  364.5 0.8 bitcast_divide_fusion
Async XLA Ops:
  12.2 114.3 %all-to-all-start = ((f32[8,128,2,1200]{1,3,2,0:T(8,128)}), f32[8,128,2,1200]{1,3,2,0:T(8,128)}, u32[]{:S(2)}, u32[]{:S(2)}) async-start(f32[8,128,2,1200]{1,3,2,0:T(8,128)} %stack.2), calls=%async_computation | async-start | bytes 19660800 | tf_op jit(solution)/shard_map/all_to_all | solution.py:10
  17.4 333.9 %reduce-scatter.2.cloned.1.call-start = ((), (), s32[]{:S(2)}) async-start(), calls=%async_computation.3 | async-start | bytes 5406720 | tf_op jit(solution)/shard_map/reduce_scatter | solution.py:19
  126.6 9.6 %copy-start = (f32[2,1200,1,1200]{3,1,2,0:T(8,128)S(1)}, f32[2,1200,1,1200]{3,1,2,0:T(8,128)}, u32[]{:S(2)}) copy-start(f32[2,1200,1,1200]{3,1,2,0:T(8,128)} %copy.12) | copy-start | bytes 34560004
  136.1 221.6 %copy-start.2 = (f32[8]{0:T(128)S(1)}, f32[8]{0:T(128)}, u32[]{:S(2)}) copy-start(f32[8]{0:T(128)} %param.8) | copy-start | bytes 100
  136.1 221.6 %copy-start.3 = (f32[4]{0:T(128)S(1)}, f32[4]{0:T(128)}, u32[]{:S(2)}) copy-start(f32[4]{0:T(128)} %param.7) | copy-start | bytes 52
  136.1 228.4 %copy-start.1 = (f32[1200]{0:T(1024)S(1)}, f32[1200]{0:T(1024)}, u32[]{:S(2)}) copy-start(f32[1200]{0:T(1024)} %param.9) | copy-start | bytes 14404
  353.0 11.5 %all-to-all-start.1 = ((f32[32,1,1200]{2,1,0:T(1,128)}), f32[32,1,1200]{2,1,0:T(1,128)S(1)}, u32[]{:S(2)}, u32[]{:S(2)}) async-start(f32[32,1,1200]{2,1,0:T(1,128)} %copy.10), calls=%async_computation.2 | async-start | bytes 327680 | tf_op jit(solution)/shard_map/all_to_all | solution.py:28
Sparse Core Ops, SparseCore 0:
  218.4 132.8 reduce-scatter.1
